TPU v7x, 128 devices: a whole 4x4x4 slice. The times are simulated.
128 devices in a mesh: row: 16 (over y, x), col: 8 (over z, core).
Axes of the slice: x: 4, y: 4, z: 4, core: 2. Of those that a mesh axis runs over, the one named last changes fastest.
Arguments:
- gain_pair: float32 [2], replicated, may hold values from 0.5 to 2
- weight_up: bfloat16 [24576, 6144], P('row', 'col'), as said below
- weight_down: bfloat16 [6144, 24576], P('row', 'col'), as said below
- inputs_up: bfloat16 [3072, 6144], P('row', 'col'), may hold values from -8 to 8, as said below
- grads_up: bfloat16 [3072, 24576], P('col', 'row'), may hold values from -0.125 to 0.125, as said below
- inputs_down: bfloat16 [3072, 24576], P('row', 'col'), may hold values from -8 to 8, as said below
- grads_down: bfloat16 [3072, 6144], P('col', 'row'), may hold values from -0.125 to 0.125, as said below
- vector_up: float32 [6144], P('col'), may hold values from -6 to 6
- vector_down: float32 [24576], P('col'), may hold values from -6 to 6
Outputs:
- wgrad_up: bfloat16 [24576, 6144], P('row', 'col')
- wgrad_down: bfloat16 [6144, 24576], P('row', 'col')
- gain_grads: float32 [2], replicated
- left_up: float32 [24576], P('row')
- right_up: float32 [6144], P('col')
- left_down: float32 [6144], P('row')
- right_down: float32 [24576], P('col')
Inputs may be any that keep to these rules, and one draw needn't show every extreme that they name: `weight_up`: drawn afresh from the seed for every entry. `weight_down`: drawn afresh from the seed for every entry. `inputs_up`: drawn afresh from the seed for every entry. `inputs_down`: drawn afresh from the seed for every entry. `grads_up`: drawn afresh from the seed for every entry. `grads_down`: drawn afresh from the seed for every entry.
All inputs are finite; a program needn't handle non-finite values.
Results may differ from a plain program's by a relative error of at most 0.007.
Values may be sent and summed in bfloat16 or wider, within the bound.
A program may use at most 128 MiB of HBM per device.

v0:
```python
import jax
import jax.numpy as jnp
from jax import lax
from jax.sharding import PartitionSpec as P

ITERS = 2


def contract(first, second):
    return lax.dot_general(
        first, second, (((0,), (0,)), ((), ())), preferred_element_type=jnp.float32
    )


def local(
    gain_pair,
    weight_up,
    weight_down,
    inputs_up,
    grads_up,
    inputs_down,
    grads_down,
    vector_up,
    vector_down,
):
    weights = (weight_up, weight_down)
    inputs_all = (
        lax.all_gather(inputs_up, "row", axis=0, tiled=True),
        lax.all_gather(inputs_down, "row", axis=0, tiled=True),
    )
    slice_up = inputs_all[0]
    slice_down = inputs_all[1]
    wsum_up = contract(lax.all_gather(grads_up, "col", axis=0, tiled=True), slice_up)
    wsum_down = contract(lax.all_gather(grads_down, "col", axis=0, tiled=True), slice_down)
    grad_ws = (wsum_up, wsum_down)
    local_inner = tuple((jnp.sum(grad_ws[k] * weights[k].astype(jnp.float32)) for k in range(2)))
    right = (vector_up, vector_down)
    lefts = right
    left_b = right
    sigma = (jnp.float32(1.0), jnp.float32(1.0))
    inner = local_inner
    for step in range(ITERS):
        right_b = tuple((right[k].astype(jnp.bfloat16) for k in range(2)))
        partial_s = tuple(
            (jnp.dot(weights[k], right_b[k], preferred_element_type=jnp.float32) for k in range(2))
        )
        prod_s = lax.psum(partial_s, "col")
        squares = lax.psum((jnp.sum(prod_s[0] * prod_s[0]), jnp.sum(prod_s[1] * prod_s[1])), "row")
        lefts = tuple((prod_s[k] / jnp.sqrt(squares[k] + 1e-06) for k in range(2)))
        left_b = tuple((lefts[k].astype(jnp.bfloat16) for k in range(2)))
        partial_t = tuple(
            (jnp.dot(left_b[k], weights[k], preferred_element_type=jnp.float32) for k in range(2))
        )
        prod_t = lax.psum(partial_t, "row")
        if step + 1 < ITERS:
            right = prod_t
        else:
            local_sq = (jnp.sum(prod_t[0] * prod_t[0]), jnp.sum(prod_t[1] * prod_t[1]))
            totals = lax.psum((local_sq[0], local_sq[1]), "col")
            inner = lax.psum(local_inner, ("row", "col"))
            sigma = tuple((jnp.sqrt(totals[k] + 1e-06) for k in range(2)))
            right = tuple((prod_t[k] / sigma[k] for k in range(2)))
    results = []
    for k in range(2):
        gain = gain_pair[k]
        outer = left_b[k].astype(jnp.float32)[:, None] * right[k][None, :]
        scaled = gain / sigma[k] * grad_ws[k] - gain * inner[k] / (sigma[k] * sigma[k]) * outer
        results.append(scaled.astype(jnp.bfloat16))
    gain_grads = jnp.stack([inner[0] / sigma[0], inner[1] / sigma[1]])
    return (results[0], results[1], gain_grads, lefts[0], right[0], lefts[1], right[1])


def solution(mesh):
    in_specs = (
        P(),
        P("row", "col"),
        P("row", "col"),
        P("row", "col"),
        P("col", "row"),
        P("row", "col"),
        P("col", "row"),
        P("col"),
        P("col"),
    )
    out_specs = (P("row", "col"), P("row", "col"), P(), P("row"), P("col"), P("row"), P("col"))
    return jax.shard_map(local, mesh=mesh, in_specs=in_specs, out_specs=out_specs, check_vma=False)
```

profile of v0, /device:TPU:1, one launch (start us, length us, event | category | flops | bytes accessed | tf_op | source)
XLA Modules:
  0.0 432.2 jit_solution(8789396443149468715)
XLA Ops:
  7.2 0.7 all-gather.7.cloned.1.call-update
  8.0 0.7 all-gather.5.cloned.1.call-update
  8.7 0.7 all-gather.9.cloned.1.call-update
  10.0 0.7 convert_element_type.42
  10.7 0.7 convert_element_type.49
  11.4 2.4 convolution_reduce_fusion.1
  13.8 0.7 convolution_reduce_fusion.5
  14.5 25.2 %all-reduce.7 = (f32[1536]{0:T(1024)S(1)}, f32[384]{0:T(512)S(1)}) all-reduce(f32[1536]{0:T(1024)S(1)} %convolution_reduce_fusion.1, f32[384]{0:T(512)S(1)} %convolution_reduce_fusion.5), channel_id=1, replica_groups=mesh['row'=16,'col'=8] {'col'}, use_global_device_ids=true, to_apply=%region_0.0 | all-reduce | flops 1920 | bytes 15360 | tf_op jit(solution)/shard_map/psum | solution.py:47
  39.8 0.6 multiply_reduce_fusion.4
  40.4 0.6 multiply_reduce_fusion.7
  41.0 35.4 %all-reduce.4 = (f32[]{:T(128)}, f32[]{:T(128)}) all-reduce(f32[]{:T(128)} %multiply_reduce_fusion.4, f32[]{:T(128)} %multiply_reduce_fusion.7), channel_id=1, replica_groups=mesh['row'=16,'col'=8] {'row'}, use_global_device_ids=true, to_apply=%region_2.0 | all-reduce | flops 2 | bytes 16 | tf_op jit(solution)/shard_map/psum | solution.py:48
  77.9 2.3 convolution_reduce_fusion.3
  80.6 55.6 %all-reduce.3 = (bf16[768]{0:T(1024)(128)(2,1)S(1)}, bf16[3072]{0:T(1024)(128)(2,1)S(1)}) all-reduce(f32[768]{0:T(1024)S(1)} %convolution_reduce_fusion.3, f32[3072]{0:T(1024)S(1)} %bitcast.26), channel_id=1, replica_groups=mesh['row'=16,'col'=8] {'row'}, use_global_device_ids=true, to_apply=%region_3.0 | all-reduce | flops 3840 | bytes 23040 | tf_op jit(solution)/shard_map/psum | solution.py:54
  136.3 2.4 convolution_reduce_fusion
  138.7 0.7 convolution_reduce_fusion.4
  139.4 44.8 %all-reduce.6 = (f32[1536]{0:T(1024)S(1)}, f32[384]{0:T(512)S(1)}) all-reduce(f32[1536]{0:T(1024)S(1)} %convolution_reduce_fusion, f32[384]{0:T(512)S(1)} %convolution_reduce_fusion.4), channel_id=1, replica_groups=mesh['row'=16,'col'=8] {'col'}, use_global_device_ids=true, to_apply=%region_4.0 | all-reduce | flops 1920 | bytes 15360 | tf_op jit(solution)/shard_map/psum | solution.py:47
  184.2 0.6 multiply_reduce_fusion.3
  184.8 0.6 multiply_reduce_fusion.6
  185.4 30.5 %all-reduce.2 = (f32[]{:T(128)}, f32[]{:T(128)}) all-reduce(f32[]{:T(128)} %multiply_reduce_fusion.3, f32[]{:T(128)} %multiply_reduce_fusion.6), channel_id=1, replica_groups=mesh['row'=16,'col'=8] {'row'}, use_global_device_ids=true, to_apply=%region_6.0 | all-reduce | flops 2 | bytes 16 | tf_op jit(solution)/shard_map/psum | solution.py:48
  217.3 0.6 fusion
  217.9 0.6 fusion.1
  218.5 2.2 convolution_reduce_fusion.2
  221.1 61.1 %all-reduce.1 = (f32[768]{0:T(1024)S(1)}, f32[3072]{0:T(1024)S(1)}) all-reduce(f32[768]{0:T(1024)S(1)} %convolution_reduce_fusion.2, f32[3072]{0:T(1024)S(1)} %bitcast.27), channel_id=1, replica_groups=mesh['row'=16,'col'=8] {'row'}, use_global_device_ids=true, to_apply=%region_7.0 | all-reduce | flops 3840 | bytes 30720 | tf_op jit(solution)/shard_map/psum | solution.py:54
  282.3 0.6 multiply_reduce_fusion.2
  282.9 0.6 multiply_reduce_fusion.5
  283.5 35.7 %all-reduce.5 = (f32[]{:T(128)}, f32[]{:T(128)}) all-reduce(f32[]{:T(128)} %multiply_reduce_fusion.5, f32[]{:T(128)} %multiply_reduce_fusion.2), channel_id=1, replica_groups=mesh['row'=16,'col'=8] {'col'}, use_global_device_ids=true, to_apply=%region_9.0 | all-reduce | flops 2 | bytes 16 | tf_op jit(solution)/shard_map/psum | solution.py:59
  322.6 14.2 %multiply_reduce_fusion.1 = (f32[]{:T(128)}, f32[1536,768]{1,0:T(8,128)}) fusion(bf16[1536,768]{1,0:T(8,128)(2,1)} %param.10, bf16[3072,1536]{1,0:T(8,128)(2,1)} %all-gather.5.cloned.1.call-done, bf16[3072,768]{1,0:T(8,128)(2,1)} %all-gather.7.cloned.1.call-done), kind=kOutput, calls=%fused_computation.3 | convolution fusion | flops 7251296256 | bytes 21233668 | tf_op jit(solution)/shard_map/dot_general | solution.py:10
  336.8 14.7 %multiply_reduce_fusion = (f32[]{:T(128)}, f32[384,3072]{1,0:T(8,128)}) fusion(bf16[384,3072]{1,0:T(8,128)(2,1)S(1)} %copy-done, bf16[3072,384]{1,0:T(8,128)(2,1)} %all-gather.9.cloned.1.call-done, bf16[3072,3072]{1,0:T(8,128)(2,1)} %all-gather.11.cloned.1.call-done), kind=kOutput, calls=%fused_computation.1 | convolution fusion | flops 7251296256 | bytes 28311556 | tf_op jit(solution)/shard_map/dot_general | solution.py:10
  351.5 62.2 %all-reduce = (f32[]{:T(128)}, f32[]{:T(128)}) all-reduce(f32[]{:T(128)} %get-tuple-element.31, f32[]{:T(128)} %get-tuple-element.33), channel_id=1, replica_groups=mesh['row'=16,'col'=8] {'row','col'}, use_global_device_ids=true, to_apply=%region_11.0 | all-reduce | flops 2 | bytes 16 | tf_op jit(solution)/shard_map/psum | solution.py:60
  417.8 0.6 pad_maximum_fusion
  418.3 4.8 %subtract_convert_fusion.1 = bf16[1536,768]{1,0:T(8,128)(2,1)} fusion(f32[1536,768]{1,0:T(8,128)} %get-tuple-element.32, f32[768]{0:T(1024)S(1)} %broadcast_divide_fusion.2, f32[1536]{0:T(1024)S(1)} %get-tuple-element.26, f32[]{:T(128)S(6)} %div.59, f32[]{:T(128)S(6)} %div.58), kind=kLoop, calls=%fused_computation.2 | loop fusion | flops 5898240 | bytes 7087112 | tf_op jit(solution)/shard_map/convert_element_type | solution.py:68
  423.1 2.5 subtract_convert_fusion
  (34 shorter events, 2.2 us)
Async XLA Ops:
  7.2 6.6 %copy-start = (bf16[384,3072]{1,0:T(8,128)(2,1)S(1)}, bf16[384,3072]{1,0:T(8,128)(2,1)}, u32[]{:S(2)}) copy-start(bf16[384,3072]{1,0:T(8,128)(2,1)} %param.11) | copy-start | bytes 7077892
  7.2 315.4 %all-gather.7.cloned.1.call-start = ((), (), s32[]{:S(2)}) async-start(), calls=%async_computation.1 | async-start | bytes 5013504 | tf_op jit(solution)/shard_map/all_gather | solution.py:28
  7.9 314.7 %all-gather.5.cloned.1.call-start = ((), (), s32[]{:S(2)}) async-start(), calls=%async_computation | async-start | bytes 10616832 | tf_op jit(solution)/shard_map/all_gather | solution.py:33
  8.7 328.1 %all-gather.9.cloned.1.call-start = ((), (), s32[]{:S(2)}) async-start(), calls=%async_computation.2 | async-start | bytes 2654208 | tf_op jit(solution)/shard_map/all_gather | solution.py:34
  9.4 327.4 %all-gather.11.cloned.1.call-start = ((), (), s32[]{:S(2)}) async-start(), calls=%async_computation.3 | async-start | bytes 20054016 | tf_op jit(solution)/shard_map/all_gather | solution.py:29
  136.3 183.6 %copy-start.4 = (f32[2]{0:T(128)S(1)}, f32[2]{0:T(128)}, u32[]{:S(2)}) copy-start(f32[2]{0:T(128)} %param.9) | copy-start | bytes 28
  322.5 95.8 %copy-start.3 = (f32[768]{0:T(1024)}, f32[768]{0:T(1024)S(1)}, u32[]{:S(2)}) copy-start(f32[768]{0:T(1024)S(1)} %broadcast_divide_fusion.2) | copy-start | bytes 9220
  322.5 100.6 %copy-start.2 = (f32[3072]{0:T(1024)}, f32[3072]{0:T(1024)S(1)}, u32[]{:S(2)}) copy-start(f32[3072]{0:T(1024)S(1)} %broadcast_divide_fusion) | copy-start | bytes 36868
  417.7 5.4 %copy-start.1 = (f32[384,3072]{1,0:T(8,128)S(1)}, f32[384,3072]{1,0:T(8,128)}, u32[]{:S(2)}) copy-start(f32[384,3072]{1,0:T(8,128)} %get-tuple-element.34) | copy-start | bytes 14155780
Sparse Core Ops, SparseCore 0:
  10.1 57.1 all-gather.6
  69.0 54.5 all-gather.4
  125.3 25.8 all-gather.8
  153.2 123.2 all-gather.10
where the time goes:
time: 433 us; the launch traced here: 432 us
  blocking collectives  351 us (81%)
  matrix products  40.5 us (9%)
  between operations  23.5 us (5%)
  other arithmetic  14.1 us (3%)
    psum x2, blocking collectives, local(): prod_t = lax.psum(partial_t, 'row')  117 us
    psum x2, blocking collectives, local(): prod_s = lax.psum(partial_s, 'col')  70 us
    psum x2, blocking collectives, local(): lax.psum((jnp.sum(prod_s[0] * prod_s[0]), jnp.sum(prod_s[1] * prod_s[1]))...  65.9 us
    psum x1, blocking collectives, local(): inner = lax.psum(local_inner, ('row', 'col'))  62.2 us
    psum x1, blocking collectives, local(): totals = lax.psum((local_sq[0], local_sq[1]), 'col')  35.7 us
    dot_general x2, matrix products, contract(): lax.dot_general(first, second, (((0,), (0,)), ((), ())), preferred_elemen...  28.9 us
  transfers between devices with their start and end apart: 4, of which 0 were waited for; matrix products, arithmetic and copies ran while one was open for 8% of the time, Pallas kernels for 0%

commit v1 on v0

v1 whole, which is shorter than its diff:
```python
import jax
import jax.numpy as jnp
from jax import lax
from jax.experimental import pallas as pl
from jax.experimental.pallas import tpu as pltpu
from jax.sharding import PartitionSpec as P

ITERS = 2
MESH = pl.DeviceIdType.MESH
F32 = jnp.float32
BF16 = jnp.bfloat16

TOK = 192
MU, MD = 1536, 384
NU, ND = 768, 3072
T = 3072
TC = 384
NALL = NU + ND
MALL = MU + MD
Q = ND // 4


def shift(i, d, n):
    return lax.rem(i + (d + n), n)


def lanes(v):
    total = v[:, 0:128]
    for k in range(128, v.shape[1], 128):
        total = total + v[:, k : k + 128]
    return total


def kernel(
    gain, wu_h, wd_h, xu_h, yu_h, xd_h, yd_h, vu_in, vd_in,
    ou, od, gg, lu, ru, ld, rd,
    xu, xd, yt, ystage, wu, wd, gu, gsend, gdown, relay, gwacc, ucol,
    e_core, e_z, e_x, e_y, f_core, f_z, f_x, f_y,
    load_sem, store_sem, as_, ar, xs, xr, ys, yr, zs, zr, os_, or_, es, er, fs, fr,
):
    row = lax.axis_index("row")
    col = lax.axis_index("col")
    y, x = lax.div(row, 4), lax.rem(row, 4)
    z, core = lax.div(col, 2), lax.rem(col, 2)

    def at_x(i):
        return {"row": y * 4 + i, "col": col}

    def at_y(i):
        return {"row": i * 4 + x, "col": col}

    def at_z(i):
        return {"row": row, "col": i * 2 + core}

    def at_core(i):
        return {"row": row, "col": z * 2 + i}

    barrier = pltpu.get_barrier_semaphore()
    for d in (1, 2, 3):
        pl.semaphore_signal(barrier, inc=1, device_id=at_x(shift(x, d, 4)), device_id_type=MESH)
        pl.semaphore_signal(barrier, inc=1, device_id=at_y(shift(y, d, 4)), device_id_type=MESH)
        pl.semaphore_signal(barrier, inc=1, device_id=at_z(shift(z, d, 4)), device_id_type=MESH)
    pl.semaphore_signal(barrier, inc=1, device_id=at_core(1 - core), device_id_type=MESH)

    def half_rows(start, size, part):
        return pl.ds(start, size) if part is None else pl.ds(start + part * (size // 2), size // 2)

    def own_half(part):
        return pl.ds(0, TOK) if part is None else pl.ds(part * (TOK // 2), TOK // 2)

    def slots(part):
        return pl.ds(0, 4) if part is None else pl.ds(part * 2, 2)

    def tokens_of(i):
        return pl.ds(pl.multiple_of((i * 2 + core) * TC, 128), TC)

    loads = [
        pltpu.make_async_copy(wu_h, wu, load_sem.at[0]),
        pltpu.make_async_copy(wd_h, wd, load_sem.at[1]),
        pltpu.make_async_copy(xd_h.at[:, pl.ds(pl.multiple_of(x * Q, 128), Q)], xd.at[y, x], load_sem.at[2]),
        pltpu.make_async_copy(xu_h, xu.at[y, x], load_sem.at[3]),
        pltpu.make_async_copy(yd_h, ystage.at[:, pl.ds(MU, MD)], load_sem.at[4]),
        pltpu.make_async_copy(yu_h, ystage.at[:, pl.ds(0, MU)], load_sem.at[5]),
    ]
    for c in (4, 2, 5, 0, 1, 3):
        loads[c].start()

    sent = []

    def remote(ref, dst_ref, send, recv, device):
        return pltpu.make_async_remote_copy(
            src_ref=ref, dst_ref=dst_ref, send_sem=send, recv_sem=recv,
            device_id=device, device_id_type=MESH,
        )

    def go(copies):
        for c in copies:
            c.start()
            sent.append(c)

    def arrived(copies):
        for c in copies:
            c.wait_recv()

    class Ring:
        def __init__(self, me, where, region, send, recv, other=None):
            up, down = where(shift(me, 1, 4)), where(shift(me, -1, 4))

            def copy(o, part, device, k):
                ref = region(o, part)
                return remote(ref, ref, send.at[k], recv.at[k], device)

            self.a = lambda: [copy(0, None, up, 0), copy(0, None, down, 1)]
            self.b = lambda: [copy(-1, 0, up, 2), copy(1, 1, down, 3)]
            self.to_other = lambda k: copy((0, -1, 1, 2)[k], None, other, 4 + k)
            self.other = other is not None

        def full(self):
            go(self.a())
            if self.other:
                go([self.to_other(0)])

        def half(self):
            arrived(self.a())
            go(self.b())
            if self.other:
                go([self.to_other(1), self.to_other(2)])

        def done(self):
            arrived(self.b())
            if self.other:
                go([self.to_other(3)])

        def fin(self):
            arrived([self.to_other(k) for k in range(4)])

    def quarter(d):
        q = shift(x, d, 4)
        return remote(
            xd_h.at[:, pl.ds(pl.multiple_of(q * Q, 128), Q)], xd.at[y, x], as_.at[d - 1], ar.at[d - 1], at_x(q)
        )

    offs = (0, -1, 1, 2)
    xd_y = [
        Ring(y, at_y, lambda o, part, s=s: xd.at[shift(y, o, 4), shift(x, s, 4), own_half(part)], ys.at[k], yr.at[k])
        for k, s in enumerate(offs)
    ]
    xu_x = Ring(x, at_x, lambda o, part: xu.at[y, shift(x, o, 4), own_half(part)], xs.at[0], xr.at[0])
    xu_y = [
        Ring(
            y, at_y, lambda o, part, j=j: xu.at[shift(y, o, 4), slots(part), :, pl.ds(j * 256, 256)],
            ys.at[4 + j], yr.at[4 + j],
        )
        for j in range(3)
    ]

    yd_x = Ring(
        x, at_x,
        lambda o, part: yt.at[0, half_rows(shift(x, o, 4) * MD, MD, part), tokens_of(z)],
        xs.at[1], xr.at[1],
    )
    other = at_core(1 - core)
    yd_z = [
        Ring(
            z, at_z,
            lambda o, part, s=s: yt.at[0, half_rows(shift(x, s, 4) * MD, MD, part), tokens_of(shift(z, o, 4))],
            zs.at[k], zr.at[k], other,
        )
        for k, s in enumerate(offs)
    ]
    yu_z = [
        Ring(
            z, at_z, lambda o, part, j=j: yt.at[1, half_rows(j * 512, 512, part), tokens_of(shift(z, o, 4))],
            zs.at[4 + j], zr.at[4 + j], other,
        )
        for j in range(3)
    ]

    def xchg(buf, n, me, where, send, recv):
        return [
            remote(buf.at[me], buf.at[me], send.at[d - 1], recv.at[d - 1], where(shift(me, d, n)))
            for d in range(1, n)
        ]

    def put(buf, n, me, where, send, recv, value):
        buf[me] = value
        copies = xchg(buf, n, me, where, send, recv)
        for c in copies:
            c.start()
            sent.append(c)
        return copies

    def get(buf, n, copies):
        for c in copies:
            c.wait_recv()
        total = buf[0]
        for k in range(1, n):
            total = total + buf[k]
        return total

    def rows16(v):
        return jnp.broadcast_to(v, (16, v.shape[1])).astype(BF16)

    state = {"vu": None, "vd": None}

    def s_send(it):
        if it == 0:
            vu, vd = vu_in[...], vd_in[...]
        else:
            vu, vd = t_fin(it - 1)
        nt = (((1,), (1,)), ((), ()))
        su = lax.dot_general(rows16(vu), wu[...], nt, preferred_element_type=F32)[0:1]
        sd = lax.dot_general(rows16(vd), wd[...], nt, preferred_element_type=F32)[0:1]
        state["c"] = put(
            e_core.at[it], 2, core, at_core, es.at[it, 0], er.at[it, 0],
            jnp.concatenate([su, sd], axis=1),
        )

    def s_z(it):
        v = get(e_core.at[it], 2, state["c"])
        state["c"] = put(e_z.at[it], 4, z, at_z, es.at[it, 1], er.at[it, 1], v)

    def t_x(it):
        s = get(e_z.at[it], 4, state["c"])
        su, sd = s[:, :MU], s[:, MU:]
        state["s"] = (su, sd)
        tu = jnp.dot(rows16(su), wu[...], preferred_element_type=F32)[0:1]
        td = jnp.dot(rows16(sd), wd[...], preferred_element_type=F32)[0:1]
        v = jnp.concatenate([tu, td, lanes(su * su), lanes(sd * sd)], axis=1)
        state["c"] = put(e_x.at[it], 4, x, at_x, es.at[it, 2], er.at[it, 2], v)

    def t_y(it):
        v = get(e_x.at[it], 4, state["c"])
        state["c"] = put(e_y.at[it], 4, y, at_y, es.at[it, 3], er.at[it, 3], v)

    def t_fin(it):
        v = get(e_y.at[it], 4, state["c"])
        nu = jnp.sqrt(jnp.sum(v[:, NALL : NALL + 128], axis=1, keepdims=True) + 1e-06)
        nd = jnp.sqrt(jnp.sum(v[:, NALL + 128 :], axis=1, keepdims=True) + 1e-06)
        tu, td = v[:, :NU] / nu, v[:, NU:NALL] / nd
        if it + 1 == ITERS:
            su, sd = state["s"]
            uu, ud = su / nu, sd / nd
            lu[...] = uu
            ld[...] = ud
            ru[...] = tu
            rd[...] = td
            ub = jnp.concatenate([uu, ud], axis=1).astype(BF16).astype(F32)
            for s in range(0, MALL, 128):
                ucol[s : s + 128, :] = jnp.broadcast_to(ub[:, s : s + 128], (128, 128)).T
        return tu, td

    def product(which, xref, m0, tm, n0):
        xs_ = xref[:, :, :, pl.ds(pl.multiple_of(n0, 128), 256)].reshape(T, 256)
        return jnp.dot(yt[which, pl.ds(pl.multiple_of(m0, 128), tm), :], xs_, preferred_element_type=F32)

    def up(m, n):
        @pl.loop(0, 2)
        def _(k):
            rows, cols = pl.ds(pl.multiple_of(m * 512 + k * 256, 128), 256), pl.ds(n * 256, 256)
            g = product(1, xu, m * 512 + k * 256, 256, n * 256)
            gu[rows, cols] = g
            prod = g * wu[rows, cols].astype(F32)
            gwacc[0] += jnp.sum(prod.reshape(32, 8, 256), axis=0)

    def out_copies(o):
        if o == 2:
            return [
                remote(gsend.at[0, pl.ds(0, 192)], relay.at[0], os_.at[0], or_.at[0], at_x(shift(x, 1, 4))),
                remote(gsend.at[0, pl.ds(192, 192)], relay.at[1], os_.at[1], or_.at[1], at_x(shift(x, -1, 4))),
            ]
        k = 2 if o == 1 else 3
        return [remote(gsend.at[k - 1], gdown.at[x], os_.at[k], or_.at[k], at_x(shift(x, o, 4)))]

    def relays():
        return [
            remote(relay.at[0], gdown.at[shift(x, -1, 4), pl.ds(0, 192)], os_.at[4], or_.at[4], at_x(shift(x, 1, 4))),
            remote(relay.at[1], gdown.at[shift(x, 1, 4), pl.ds(192, 192)], os_.at[5], or_.at[5], at_x(shift(x, -1, 4))),
        ]

    def down(o):
        dst = gdown.at[x] if o == 0 else gsend.at[{2: 0, 1: 1, -1: 2}[o]]

        @pl.loop(0, Q // 256)
        def _(k):
            g = product(0, xd, shift(x, o, 4) * MD, MD, k * 256)
            dst[:, pl.ds(pl.multiple_of(k * 256, 128), 256)] = g.astype(BF16)

        if o != 0:
            go(out_copies(o))

    def pass_on():
        arrived(out_copies(2))
        go(relays())

    def inner_down():
        arrived(out_copies(1) + out_copies(-1) + relays())

        @pl.loop(0, 4)
        def _(q):
            for r in range(0, MD, 128):
                cols = pl.ds(pl.multiple_of(q * Q, 128), Q)
                prod = gdown[q, r : r + 128, :].astype(F32) * wd[r : r + 128, cols].astype(F32)
                acc = jnp.sum(prod.reshape(16, 8, Q), axis=0)
                gwacc[1] += acc[:, 0:256] + acc[:, 256:512] + acc[:, 512:768]

    gwacc[...] = jnp.zeros_like(gwacc)
    pl.semaphore_wait(barrier, 10)
    go([quarter(1), quarter(3)])
    loads[4].wait()
    yt[0, pl.ds(pl.multiple_of(x * MD, 128), MD), tokens_of(z)] = ystage[:, MU:].T
    yd_x.full()
    yd_z[0].full()
    loads[2].wait()
    xd_y[0].full()
    go([quarter(2)])
    loads[0].wait()
    loads[1].wait()
    s_send(0)
    loads[5].wait()
    for s in range(0, MU, 384):
        yt[1, s : s + 384, tokens_of(z)] = ystage[:, s : s + 384].T
    arrived([quarter(1), quarter(3)])
    xd_y[1].full()
    yd_x.half()
    yd_z[1].full()
    xd_y[0].half()
    yd_z[0].half()
    s_z(0)
    xd_y[2].full()
    yd_z[2].full()
    loads[3].wait()
    xu_x.full()
    xd_y[1].half()
    yd_z[1].half()
    xd_y[0].done()
    yd_z[0].done()
    t_x(0)
    arrived([quarter(2)])
    xd_y[3].full()
    yd_x.done()
    yd_z[3].full()
    xd_y[2].half()
    yd_z[2].half()
    xd_y[1].done()
    yd_z[1].done()
    t_y(0)
    xu_x.half()
    xu_x.done()
    xu_y[0].full()
    yu_z[0].full()
    xd_y[3].half()
    yd_z[3].half()
    xd_y[2].done()
    yd_z[2].done()
    s_send(1)
    s_z(1)
    xu_y[1].full()
    yu_z[1].full()
    xd_y[3].done()
    yd_z[3].done()
    for r in yd_z:
        r.fin()
    xu_y[0].half()
    yu_z[0].half()
    down(2)
    t_x(1)
    down(1)
    down(-1)
    xu_y[2].full()
    yu_z[2].full()
    t_y(1)
    down(0)
    pass_on()
    xu_y[1].half()
    yu_z[1].half()
    xu_y[0].done()
    yu_z[0].done()
    yu_z[0].fin()
    up(0, 0)
    t_fin(1)
    xu_y[2].half()
    yu_z[2].half()
    xu_y[1].done()
    yu_z[1].done()
    yu_z[1].fin()
    up(0, 1)
    up(1, 1)
    up(1, 0)
    inner_down()
    xu_y[2].done()
    yu_z[2].done()
    up(0, 2)
    up(1, 2)
    yu_z[2].fin()
    up(2, 0)
    up(2, 1)
    up(2, 2)

    gw = jnp.concatenate(
        [lanes(jnp.sum(gwacc[k], axis=0, keepdims=True)) for k in range(2)], axis=1
    )
    c = put(f_x, 4, x, at_x, fs.at[0], fr.at[0], gw)
    gw = get(f_x, 4, c)
    c = put(f_y, 4, y, at_y, fs.at[1], fr.at[1], gw)
    gw = get(f_y, 4, c)
    tu, td = ru[...], rd[...]
    both = jnp.concatenate([gw, lanes(tu * tu), lanes(td * td)], axis=1)
    c = put(f_core, 2, core, at_core, fs.at[2], fr.at[2], both)
    both = get(f_core, 2, c)
    c = put(f_z, 4, z, at_z, fs.at[3], fr.at[3], both)
    both = get(f_z, 4, c)

    def total(k):
        return jnp.sum(both[:, k * 128 : k * 128 + 128], axis=1, keepdims=True)

    stores = []
    for k, (rref, t, w, out) in enumerate(((ru, tu, wu, ou), (rd, td, wd, od))):
        inner = total(k)
        sigma = jnp.sqrt(total(2 + k) + 1e-06)
        v = t / sigma
        rref[...] = v
        gg[:, k * 128 : k * 128 + 128] = jnp.broadcast_to(inner / sigma, (1, 128))
        first = gain[k] / sigma
        second = gain[k] * inner / (sigma * sigma)

        if k == 0:

            @pl.loop(0, MU // 128)
            def _(r):
                rows = pl.ds(pl.multiple_of(r * 128, 128), 128)
                u = ucol[rows, :] * second
                for c0 in range(0, NU, 128):
                    cols = pl.ds(c0, 128)
                    w[rows, cols] = (first * gu[rows, cols] - u * v[:, c0 : c0 + 128]).astype(BF16)

        else:

            @pl.loop(0, MD // 128)
            def _(r):
                rows = pl.ds(pl.multiple_of(r * 128, 128), 128)
                u = ucol[pl.ds(pl.multiple_of(MU + r * 128, 128), 128), :] * second
                for q in range(4):
                    for c0 in range(0, Q, 128):
                        n0 = q * Q + c0
                        g = gdown[q, rows, c0 : c0 + 128].astype(F32)
                        w[rows, n0 : n0 + 128] = (first * g - u * v[:, n0 : n0 + 128]).astype(BF16)

        c = pltpu.make_async_copy(w, out, store_sem.at[k])
        c.start()
        stores.append(c)
    for c in sent:
        c.wait_send()
    for c in stores:
        c.wait()


def local(gain_pair, weight_up, weight_down, inputs_up, grads_up, inputs_down, grads_down, vector_up, vector_down):
    hbm = pl.BlockSpec(memory_space=pl.ANY)
    vmem = pl.BlockSpec(memory_space=pltpu.VMEM)
    dma = pltpu.SemaphoreType.DMA
    ou, od, gg, lu, ru, ld, rd = pl.pallas_call(
        kernel,
        out_shape=(
            jax.ShapeDtypeStruct((MU, NU), BF16),
            jax.ShapeDtypeStruct((MD, ND), BF16),
            jax.ShapeDtypeStruct((1, 256), F32),
            jax.ShapeDtypeStruct((1, MU), F32),
            jax.ShapeDtypeStruct((1, NU), F32),
            jax.ShapeDtypeStruct((1, MD), F32),
            jax.ShapeDtypeStruct((1, ND), F32),
        ),
        in_specs=[pl.BlockSpec(memory_space=pltpu.SMEM)] + [hbm] * 6 + [vmem] * 2,
        out_specs=(hbm, hbm) + (vmem,) * 5,
        scratch_shapes=[
            pltpu.VMEM((4, 4, TOK, NU), BF16),
            pltpu.VMEM((4, 4, TOK, Q), BF16),
            pltpu.VMEM((2, MU, T), BF16),
            pltpu.VMEM((TC, MALL), BF16),
            pltpu.VMEM((MU, NU), BF16),
            pltpu.VMEM((MD, ND), BF16),
            pltpu.VMEM((MU, NU), F32),
            pltpu.VMEM((3, MD, Q), BF16),
            pltpu.VMEM((4, MD, Q), BF16),
            pltpu.VMEM((2, MD // 2, Q), BF16),
            pltpu.VMEM((2, 8, 256), F32),
            pltpu.VMEM((MALL, 128), F32),
            pltpu.VMEM((ITERS, 2, 1, MALL), F32),
            pltpu.VMEM((ITERS, 4, 1, MALL), F32),
            pltpu.VMEM((ITERS, 4, 1, NALL + 256), F32),
            pltpu.VMEM((ITERS, 4, 1, NALL + 256), F32),
            pltpu.VMEM((2, 1, 512), F32),
            pltpu.VMEM((4, 1, 512), F32),
            pltpu.VMEM((4, 1, 256), F32),
            pltpu.VMEM((4, 1, 256), F32),
            dma((6,)),
            dma((2,)),
            dma((3,)),
            dma((3,)),
            dma((2, 4)),
            dma((2, 4)),
            dma((7, 4)),
            dma((7, 4)),
            dma((7, 8)),
            dma((7, 8)),
            dma((6,)),
            dma((6,)),
            dma((ITERS, 4, 3)),
            dma((ITERS, 4, 3)),
            dma((4, 3)),
            dma((4, 3)),
        ],
        compiler_params=pltpu.CompilerParams(
            collective_id=0, has_side_effects=True, vmem_limit_bytes=66 * 1024 * 1024 - 3 * 1024 * 1024
        ),
    )(
        gain_pair, weight_up, weight_down, inputs_up, grads_up, inputs_down, grads_down,
        vector_up.reshape(1, NU), vector_down.reshape(1, ND),
    )
    return (
        ou, od, jnp.stack([gg[0, 0], gg[0, 128]]),
        lu.reshape(MU), ru.reshape(NU), ld.reshape(MD), rd.reshape(ND),
    )


def solution(mesh):
    in_specs = (
        P(), P("row", "col"), P("row", "col"), P("row", "col"), P("col", "row"),
        P("row", "col"), P("col", "row"), P("col"), P("col"),
    )
    out_specs = (P("row", "col"), P("row", "col"), P(), P("row"), P("col"), P("row"), P("col"))
    return jax.shard_map(local, mesh=mesh, in_specs=in_specs, out_specs=out_specs, check_vma=False)
```

time: 433 us -> 136 us (0.31)
  blocking collectives: 351 us -> 0 us
  Pallas kernels: 0 us -> 121 us
  matrix products: 40.5 us -> 0 us
  between operations: 23.5 us -> 0.65 us
  other arithmetic: 14.1 us -> 5.73 us
  local copies, waits for them, and re-layouts: 0.66 us -> 7.83 us
    psum x8 -> x0, blocking collectives: 351 us -> none  [the longest x2 117 us: local(): prod_t = lax.psum(partial_t, 'row')]
    pallas_call x0 -> x1, Pallas kernels: none -> 121 us  [local(): pl.pallas_call(kernel, out_shape=(jax.ShapeDtypeStruct((MU, NU), BF16), j...]
    dot_general x10 -> x0, matrix products: 40.5 us -> none  [the longest x2 28.9 us: contract(): lax.dot_general(first, second, (((0,), (0,)), ((), ())), preferred_elemen...]
    convert_element_type x8 -> x0, other arithmetic: 9.92 us -> none  [the longest x2 7.31 us: local(): results.append(scaled.astype(jnp.bfloat16))]
    unnamed x10 -> x7, local copies, waits for them, and re-layouts: 0.03 us -> 5.38 us
  transfers between devices with their start and end apart: 4 -> 0, of which waited for: 0 -> 0; matrix products, arithmetic and copies ran while one was open for 8% -> 0% of each run, Pallas kernels for 0% -> 0%
where the time goes in v1:
time: 136 us; the launch traced here: 135 us
  Pallas kernels  121 us (89%)
  local copies, waits for them, and re-layouts  7.83 us (6%)
  other arithmetic  5.73 us (4%)
    pallas_call x1, Pallas kernels, local(): pl.pallas_call(kernel, out_shape=(jax.ShapeDtypeStruct((MU, NU), BF16), j...  121 us
    unnamed x7, local copies, waits for them, and re-layouts  5.38 us
    pallas_call x3, other arithmetic, local(): pl.pallas_call(kernel, out_shape=(jax.ShapeDtypeStruct((MU, NU), BF16), j...  3.85 us

profile of v1, /device:TPU:1, one launch (start us, length us, event | category | flops | bytes accessed | tf_op | source)
XLA Modules:
  0.0 135.2 jit_solution(9164147007913297031)
XLA Ops:
  0.6 1.3 reshape.32.vu_in
  1.9 121.0 %shard_map.144 = (bf16[1536,768]{1,0:T(8,128)(2,1)}, bf16[384,3072]{1,0:T(8,128)(2,1)}, f32[1,256]{1,0:T(1,128)}, f32[1,1536]{1,0:T(1,128)}, f32[1,768]{1,0:T(1,...) custom-call(f32[2]{0:T(128)} %gain.1, bf16[1536,768]{1,0:T(8,128)(2,1)} %wu_h.1, bf16[384,3072]{1,0:T(8,128)(2,1)} %wd_h.1, ...), custom_call_target="tpu_custom_call" | custom-call | tf_op jit(solution)/shard_map/pallas_call | solution.py:462
  122.9 1.2 fusion
  124.1 1.9 %pad_maximum_fusion = f32[2]{0:T(128)} fusion(f32[1]{0:T(128)} %bitcast.2, f32[1]{0:T(128)} %bitcast.1), kind=kLoop, calls=%fused_computation | loop fusion | flops 2 | bytes 16 | tf_op jit(solution)/shard_map/stack | solution.py:521
  126.0 1.3 reduce
  127.3 1.3 reduce.1
  128.6 1.3 reduce.2
  129.8 0.0 copy-start
  129.8 3.4 %copy.19 = bf16[1536,768]{1,0:T(8,128)(2,1)} copy(bf16[1536,768]{1,0:T(8,128)(2,1)} %get-tuple-element.30) | data formatting | bytes 4718592
  133.2 0.0 copy-done
  133.2 0.0 copy-start.1
  133.2 1.4 %copy.20 = bf16[384,3072]{1,0:T(8,128)(2,1)} copy(bf16[384,3072]{1,0:T(8,128)(2,1)S(1)} %copy-done) | data formatting | bytes 4718592
  134.6 0.0 copy-done.1
  134.6 0.6 copy.21
Async XLA Ops:
  129.8 3.4 %copy-start = (bf16[384,3072]{1,0:T(8,128)(2,1)S(1)}, bf16[384,3072]{1,0:T(8,128)(2,1)}, u32[]{:S(2)}) copy-start(bf16[384,3072]{1,0:T(8,128)(2,1)} %get-tuple-element.31) | copy-start | bytes 7077892
  133.2 1.4 %copy-start.1 = (f32[1,3072]{1,0:T(1,128)S(1)}, f32[1,3072]{1,0:T(1,128)}, u32[]{:S(2)}) copy-start(f32[1,3072]{1,0:T(1,128)} %get-tuple-element.20) | copy-start | bytes 36868

commit v2 on v1

--- a/solution.py
+++ b/solution.py
@@ -32,11 +32,11 @@
 
 
 def kernel(
-    gain, wu_h, wd_h, xu_h, yu_h, xd_h, yd_h, vu_in, vd_in,
-    ou, od, gg, lu, ru, ld, rd,
-    xu, xd, yt, ystage, wu, wd, gu, gsend, gdown, relay, gwacc, ucol,
-    e_core, e_z, e_x, e_y, f_core, f_z, f_x, f_y,
-    load_sem, store_sem, as_, ar, xs, xr, ys, yr, zs, zr, os_, or_, es, er, fs, fr,
+    wu_h, wd_h, xu_h, yu_h, xd_h, yd_h, vu_in, vd_in,
+    gu, gdown, ucol, urow, trow, sums,
+    xu, xd, yt, ystage, wu, wd, gsend, relay, gwacc,
+    e_core, e_z, e_x, e_y, f_t, f_x, f_y, f_c,
+    load_sem, as_, ar, xs, xr, ys, yr, zs, zr, os_, or_, es, er, fs, fr,
 ):
     row = lax.axis_index("row")
     col = lax.axis_index("col")
@@ -55,12 +55,15 @@
     def at_core(i):
         return {"row": row, "col": z * 2 + i}
 
+    def at_col(i):
+        return {"row": row, "col": i}
+
     barrier = pltpu.get_barrier_semaphore()
     for d in (1, 2, 3):
         pl.semaphore_signal(barrier, inc=1, device_id=at_x(shift(x, d, 4)), device_id_type=MESH)
         pl.semaphore_signal(barrier, inc=1, device_id=at_y(shift(y, d, 4)), device_id_type=MESH)
-        pl.semaphore_signal(barrier, inc=1, device_id=at_z(shift(z, d, 4)), device_id_type=MESH)
-    pl.semaphore_signal(barrier, inc=1, device_id=at_core(1 - core), device_id_type=MESH)
+    for d in range(1, 8):
+        pl.semaphore_signal(barrier, inc=1, device_id=at_col(shift(col, d, 8)), device_id_type=MESH)
 
     def half_rows(start, size, part):
         return pl.ds(start, size) if part is None else pl.ds(start + part * (size // 2), size // 2)
@@ -205,7 +208,7 @@
 
     def s_send(it):
         if it == 0:
-            vu, vd = vu_in[...], vd_in[...]
+            vu, vd = vu_in[...].reshape(1, NU), vd_in[...].reshape(1, ND)
         else:
             vu, vd = t_fin(it - 1)
         nt = (((1,), (1,)), ((), ()))
@@ -241,13 +244,14 @@
         if it + 1 == ITERS:
             su, sd = state["s"]
             uu, ud = su / nu, sd / nd
-            lu[...] = uu
-            ld[...] = ud
-            ru[...] = tu
-            rd[...] = td
-            ub = jnp.concatenate([uu, ud], axis=1).astype(BF16).astype(F32)
+            u = jnp.concatenate([uu, ud], axis=1)
+            urow[...] = u
+            trow[...] = jnp.concatenate([tu, td], axis=1)
+            ub = u.astype(BF16).astype(F32)
             for s in range(0, MALL, 128):
                 ucol[s : s + 128, :] = jnp.broadcast_to(ub[:, s : s + 128], (128, 128)).T
+            squares = jnp.concatenate([lanes(tu * tu), lanes(td * td)], axis=1)
+            state["t"] = put(f_t, 8, col, at_col, fs.at[3], fr.at[3], squares)
         return tu, td
 
     def product(which, xref, m0, tm, n0):
@@ -305,7 +309,7 @@
                 gwacc[1] += acc[:, 0:256] + acc[:, 256:512] + acc[:, 512:768]
 
     gwacc[...] = jnp.zeros_like(gwacc)
-    pl.semaphore_wait(barrier, 10)
+    pl.semaphore_wait(barrier, 13)
     go([quarter(1), quarter(3)])
     loads[4].wait()
     yt[0, pl.ds(pl.multiple_of(x * MD, 128), MD), tokens_of(z)] = ystage[:, MU:].T
@@ -397,60 +401,61 @@
     up(2, 1)
     up(2, 2)
 
+    squares = get(f_t, 8, state["t"])
     gw = jnp.concatenate(
         [lanes(jnp.sum(gwacc[k], axis=0, keepdims=True)) for k in range(2)], axis=1
     )
-    c = put(f_x, 4, x, at_x, fs.at[0], fr.at[0], gw)
-    gw = get(f_x, 4, c)
-    c = put(f_y, 4, y, at_y, fs.at[1], fr.at[1], gw)
-    gw = get(f_y, 4, c)
-    tu, td = ru[...], rd[...]
-    both = jnp.concatenate([gw, lanes(tu * tu), lanes(td * td)], axis=1)
-    c = put(f_core, 2, core, at_core, fs.at[2], fr.at[2], both)
-    both = get(f_core, 2, c)
-    c = put(f_z, 4, z, at_z, fs.at[3], fr.at[3], both)
-    both = get(f_z, 4, c)
-
+    for k, (buf, n, me, where) in enumerate(((f_x, 4, x, at_x), (f_y, 4, y, at_y), (f_c, 8, col, at_col))):
+        gw = get(buf, n, put(buf, n, me, where, fs.at[k], fr.at[k], gw))
+    sums[...] = jnp.concatenate([gw, squares], axis=1)
+    for c in sent:
+        c.wait_send()
+
+
+def scale(gain, gu, gdown, ucol, urow, trow, sums, ou, od, gg, lu, ru, ld, rd, su, sd, sem):
     def total(k):
-        return jnp.sum(both[:, k * 128 : k * 128 + 128], axis=1, keepdims=True)
-
-    stores = []
-    for k, (rref, t, w, out) in enumerate(((ru, tu, wu, ou), (rd, td, wd, od))):
+        return jnp.sum(sums[:, k * 128 : k * 128 + 128], axis=1, keepdims=True)
+
+    def factors(k):
         inner = total(k)
         sigma = jnp.sqrt(total(2 + k) + 1e-06)
-        v = t / sigma
-        rref[...] = v
-        gg[:, k * 128 : k * 128 + 128] = jnp.broadcast_to(inner / sigma, (1, 128))
-        first = gain[k] / sigma
-        second = gain[k] * inner / (sigma * sigma)
-
-        if k == 0:
-
-            @pl.loop(0, MU // 128)
-            def _(r):
-                rows = pl.ds(pl.multiple_of(r * 128, 128), 128)
-                u = ucol[rows, :] * second
-                for c0 in range(0, NU, 128):
-                    cols = pl.ds(c0, 128)
-                    w[rows, cols] = (first * gu[rows, cols] - u * v[:, c0 : c0 + 128]).astype(BF16)
-
-        else:
-
-            @pl.loop(0, MD // 128)
-            def _(r):
-                rows = pl.ds(pl.multiple_of(r * 128, 128), 128)
-                u = ucol[pl.ds(pl.multiple_of(MU + r * 128, 128), 128), :] * second
-                for q in range(4):
-                    for c0 in range(0, Q, 128):
-                        n0 = q * Q + c0
-                        g = gdown[q, rows, c0 : c0 + 128].astype(F32)
-                        w[rows, n0 : n0 + 128] = (first * g - u * v[:, n0 : n0 + 128]).astype(BF16)
-
-        c = pltpu.make_async_copy(w, out, store_sem.at[k])
+        gg[k] = (inner / sigma)[0, 0]
+        return sigma, gain[k] / sigma, gain[k] * inner / (sigma * sigma)
+
+    stores = []
+
+    def store(src, dst):
+        c = pltpu.make_async_copy(src, dst, sem.at[len(stores)])
         c.start()
         stores.append(c)
-    for c in sent:
-        c.wait_send()
+
+    sigma, first, second = factors(0)
+    v = trow[:, :NU] / sigma
+    ru[...] = v.reshape(NU)
+    lu[...] = urow[:, :MU].reshape(MU)
+    for r0 in range(0, MU, 384):
+
+        @pl.loop(0, 3)
+        def _(r):
+            rows = pl.ds(pl.multiple_of(r0 + r * 128, 128), 128)
+            u = ucol[rows, :] * second
+            for c0 in range(0, NU, 128):
+                cols = pl.ds(c0, 128)
+                su[rows, cols] = (first * gu[rows, cols] - u * v[:, c0 : c0 + 128]).astype(BF16)
+
+        store(su.at[pl.ds(r0, 384)], ou.at[pl.ds(r0, 384)])
+
+    sigma, first, second = factors(1)
+    v = trow[:, NU:] / sigma
+    rd[...] = v.reshape(ND)
+    ld[...] = urow[:, MU:].reshape(MD)
+    for r0 in range(0, MD, 128):
+        rows = pl.ds(r0, 128)
+        u = ucol[MU + r0 : MU + r0 + 128, :] * second
+        for n0 in range(0, ND, 128):
+            g = gdown[n0 // Q, rows, n0 % Q : n0 % Q + 128].astype(F32)
+            sd[rows, n0 : n0 + 128] = (first * g - u * v[:, n0 : n0 + 128]).astype(BF16)
+        store(sd.at[rows], od.at[rows])
     for c in stores:
         c.wait()
 
@@ -458,20 +463,20 @@
 def local(gain_pair, weight_up, weight_down, inputs_up, grads_up, inputs_down, grads_down, vector_up, vector_down):
     hbm = pl.BlockSpec(memory_space=pl.ANY)
     vmem = pl.BlockSpec(memory_space=pltpu.VMEM)
+    smem = pl.BlockSpec(memory_space=pltpu.SMEM)
     dma = pltpu.SemaphoreType.DMA
-    ou, od, gg, lu, ru, ld, rd = pl.pallas_call(
+    parts = pl.pallas_call(
         kernel,
         out_shape=(
-            jax.ShapeDtypeStruct((MU, NU), BF16),
-            jax.ShapeDtypeStruct((MD, ND), BF16),
-            jax.ShapeDtypeStruct((1, 256), F32),
-            jax.ShapeDtypeStruct((1, MU), F32),
-            jax.ShapeDtypeStruct((1, NU), F32),
-            jax.ShapeDtypeStruct((1, MD), F32),
-            jax.ShapeDtypeStruct((1, ND), F32),
+            pltpu.VMEM((MU, NU), F32),
+            pltpu.VMEM((4, MD, Q), BF16),
+            pltpu.VMEM((MALL, 128), F32),
+            pltpu.VMEM((1, MALL), F32),
+            pltpu.VMEM((1, NALL), F32),
+            pltpu.VMEM((1, 512), F32),
         ),
-        in_specs=[pl.BlockSpec(memory_space=pltpu.SMEM)] + [hbm] * 6 + [vmem] * 2,
-        out_specs=(hbm, hbm) + (vmem,) * 5,
+        in_specs=[hbm] * 6 + [vmem] * 2,
+        out_specs=(vmem,) * 6,
         scratch_shapes=[
             pltpu.VMEM((4, 4, TOK, NU), BF16),
             pltpu.VMEM((4, 4, TOK, Q), BF16),
@@ -479,22 +484,18 @@
             pltpu.VMEM((TC, MALL), BF16),
             pltpu.VMEM((MU, NU), BF16),
             pltpu.VMEM((MD, ND), BF16),
-            pltpu.VMEM((MU, NU), F32),
             pltpu.VMEM((3, MD, Q), BF16),
-            pltpu.VMEM((4, MD, Q), BF16),
             pltpu.VMEM((2, MD // 2, Q), BF16),
             pltpu.VMEM((2, 8, 256), F32),
-            pltpu.VMEM((MALL, 128), F32),
             pltpu.VMEM((ITERS, 2, 1, MALL), F32),
             pltpu.VMEM((ITERS, 4, 1, MALL), F32),
             pltpu.VMEM((ITERS, 4, 1, NALL + 256), F32),
             pltpu.VMEM((ITERS, 4, 1, NALL + 256), F32),
-            pltpu.VMEM((2, 1, 512), F32),
-            pltpu.VMEM((4, 1, 512), F32),
+            pltpu.VMEM((8, 1, 256), F32),
             pltpu.VMEM((4, 1, 256), F32),
             pltpu.VMEM((4, 1, 256), F32),
+            pltpu.VMEM((8, 1, 256), F32),
             dma((6,)),
-            dma((2,)),
             dma((3,)),
             dma((3,)),
             dma((2, 4)),
@@ -507,19 +508,34 @@
             dma((6,)),
             dma((ITERS, 4, 3)),
             dma((ITERS, 4, 3)),
-            dma((4, 3)),
-            dma((4, 3)),
+            dma((4, 7)),
+            dma((4, 7)),
         ],
         compiler_params=pltpu.CompilerParams(
-            collective_id=0, has_side_effects=True, vmem_limit_bytes=66 * 1024 * 1024 - 3 * 1024 * 1024
+            collective_id=0, has_side_effects=True, vmem_limit_bytes=48 * 1024 * 1024
         ),
-    )(
-        gain_pair, weight_up, weight_down, inputs_up, grads_up, inputs_down, grads_down,
-        vector_up.reshape(1, NU), vector_down.reshape(1, ND),
-    )
-    return (
-        ou, od, jnp.stack([gg[0, 0], gg[0, 128]]),
-        lu.reshape(MU), ru.reshape(NU), ld.reshape(MD), rd.reshape(ND),
+    )(weight_up, weight_down, inputs_up, grads_up, inputs_down, grads_down, vector_up, vector_down)
+    return tuple(
+        pl.pallas_call(
+            scale,
+            out_shape=(
+                jax.ShapeDtypeStruct((MU, NU), BF16),
+                jax.ShapeDtypeStruct((MD, ND), BF16),
+                jax.ShapeDtypeStruct((2,), F32),
+                jax.ShapeDtypeStruct((MU,), F32),
+                jax.ShapeDtypeStruct((NU,), F32),
+                jax.ShapeDtypeStruct((MD,), F32),
+                jax.ShapeDtypeStruct((ND,), F32),
+            ),
+            in_specs=[smem] + [vmem] * 6,
+            out_specs=(hbm, hbm, smem) + (vmem,) * 4,
+            scratch_shapes=[
+                pltpu.VMEM((MU, NU), BF16),
+                pltpu.VMEM((MD, ND), BF16),
+                dma((7,)),
+            ],
+            compiler_params=pltpu.CompilerParams(vmem_limit_bytes=24 * 1024 * 1024),
+        )(gain_pair, *parts)
     )
 
 

time: 136 us -> 123 us (0.904)
  local copies, waits for them, and re-layouts: 7.83 us -> 0.01 us
  other arithmetic: 5.73 us -> 0 us
    unnamed x7 -> x2, local copies, waits for them, and re-layouts: 5.38 us -> 0.01 us
    pallas_call x3 -> x0, other arithmetic: 3.85 us -> none  [local(): pl.pallas_call(kernel, out_shape=(jax.ShapeDtypeStruct((MU, NU), BF16), j...]
    another operation x1 -> x0, other arithmetic: 1.88 us -> none  [local(): jnp.stack([gg[0, 0], gg[0, 128]])]
    pallas_call x1 -> x2, Pallas kernels: 121 us -> 122 us  [the longest x1 118 us: local(): pl.pallas_call(kernel, out_shape=(pltpu.VMEM((MU, NU), F32), pltpu.VMEM((...]
where the time goes in v2:
time: 123 us
  Pallas kernels  122 us (99%)
    pallas_call x1, Pallas kernels, local(): pl.pallas_call(kernel, out_shape=(pltpu.VMEM((MU, NU), F32), pltpu.VMEM((...  118 us
    pallas_call x1, Pallas kernels, local(): pl.pallas_call(scale, out_shape=(jax.ShapeDtypeStruct((MU, NU), BF16), ja...  4.02 us

profile of v2, /device:TPU:1, one launch (start us, length us, event | category | flops | bytes accessed | tf_op | source)
XLA Modules:
  0.0 122.8 jit_solution(10152622099375665359)
XLA Ops:
  0.6 0.0 copy-start
  0.6 118.0 %shard_map.144 = (f32[1536,768]{1,0:T(8,128)S(1)}, bf16[4,384,768]{2,1,0:T(8,128)(2,1)S(1)}, f32[1920,128]{1,0:T(8,128)S(1)}, f32[1,1920]{1,0:T(1,128)S(1)}, f32...) custom-call(bf16[1536,768]{1,0:T(8,128)(2,1)} %wu_h.1, bf16[384,3072]{1,0:T(8,128)(2,1)} %wd_h.1, bf16[192,768]{1,0:T(8,128)(2,1)} %xu_h.1, ...), custom_call_target="tpu_custom_call" | custom-call | tf_op jit(solution)/shard_map/pallas_call | solution.py:468
  118.7 0.0 copy-done
  118.7 4.0 %shard_map.145 = (bf16[1536,768]{1,0:T(8,128)(2,1)}, bf16[384,3072]{1,0:T(8,128)(2,1)}, f32[2]{0:T(128)}, f32[1536]{0:T(1024)}, f32[768]{0:T(1024)}, /*index=5*/f32[384]{0:T(512)}, f32[3072]{0:T(1024)}) custom-call(f32[2]{0:T(128)S(1)} %copy-done, f32[1536,768]{1,0:T(8,128)S(1)} %get-tuple-element.13.gu, bf16[4,384,768]{2,1,0:T(8,128)(2,1)S(1)} %get-tuple-element.14.gdown, ...), custom_call_target="tpu_custom_call" | custom-call | tf_op jit(solution)/shard_map/pallas_call | solution.py:519
Async XLA Ops:
  0.6 118.0 %copy-start = (f32[2]{0:T(128)S(1)}, f32[2]{0:T(128)}, u32[]{:S(2)}) copy-start(f32[2]{0:T(128)} %gain.1) | copy-start | bytes 28

commit v3 on v2

--- a/solution.py
+++ b/solution.py
@@ -18,6 +18,20 @@
 NALL = NU + ND
 MALL = MU + MD
 Q = ND // 4
+UP_GROUPS = ((0, 512), (512, 512), (1024, 384), (1408, 128))
+XFIRST = 256
+ORDER = (
+    "q13", "by_f", "dz_f", "xd0_f", "turnU", "dw0_f", "zu0_f", "dz_h", "s_send0", "ydx_f", "q13w", "xd2_f",
+    "zu3_f", "dw0_h", "s_z0", "by_h", "dw2_f", "xd1_f", "ydx_h", "q2", "zd1_f", "dz_d", "dw0_d", "xd2_h",
+    "zu0_h", "dw1_f", "zu3_h", "by_d", "ydx_d", "t_x0", "zd1_h", "q2f", "zd3_f", "dw1_h", "xd0_h", "dw2_h",
+    "t_y0", "q2w", "xd3_f", "xux_f", "zu0_d", "zu3_d", "dw3_f", "zu2_f", "xd2_d", "dw1_d", "s_send1", "zd1_d",
+    "xd1_h", "zd3_h", "xux_h", "dw2_d", "dw3_h", "s_z1", "xd3_h", "bx_f", "dw0_n", "dw1_n", "zd2_f", "zd3_d",
+    "zd1_n", "xux_d", "yu0_f", "zd0_f", "t_x1", "dw3_d", "xd0_d", "dw2_n", "xd1_d", "zd3_n", "zd2_h", "zu0_n",
+    "xd3_d", "dw3_n", "zu2_h", "zu3_n", "yu1_f", "bx_h", "down2", "zd2_d", "zd0_h", "zu1_f", "down3", "bx_d",
+    "zu2_d", "t_y1", "yu0_h", "zd2_n", "down1", "zd0_d", "up0_2", "yu1_h", "zu2_n", "t_fin1", "up3_2",
+    "up2_2", "zd0_n", "pass_on", "yu0_d", "up3_0", "zu1_h", "down0", "up0_0", "yu1_d", "up3_1", "zu1_d",
+    "up2_1", "up2_0", "up0_1", "zu1_n", "up1_2", "up1_1", "up1_0", "inner_down",
+)
 
 
 def shift(i, d, n):
@@ -34,7 +48,7 @@
 def kernel(
     wu_h, wd_h, xu_h, yu_h, xd_h, yd_h, vu_in, vd_in,
     gu, gdown, ucol, urow, trow, sums,
-    xu, xd, yt, ystage, wu, wd, gsend, relay, gwacc,
+    xu, xd, yt, ystage, wu, wd, gsend, relay, qrelay, gwacc,
     e_core, e_z, e_x, e_y, f_t, f_x, f_y, f_c,
     load_sem, as_, ar, xs, xr, ys, yr, zs, zr, os_, or_, es, er, fs, fr,
 ):
@@ -143,40 +157,77 @@
             xd_h.at[:, pl.ds(pl.multiple_of(q * Q, 128), Q)], xd.at[y, x], as_.at[d - 1], ar.at[d - 1], at_x(q)
         )
 
+    def far_quarter():
+        cols = pl.ds(pl.multiple_of(shift(x, 2, 4) * Q, 128), Q)
+        return [
+            remote(xd_h.at[own_half(k), cols], qrelay.at[k], as_.at[k + 3], ar.at[k + 3], at_x(shift(x, d, 4)))
+            for k, d in enumerate((1, -1))
+        ]
+
+    def far_quarter_relays():
+        return [
+            remote(
+                qrelay.at[k], xd.at[y, shift(x, -d, 4), own_half(k)], as_.at[k + 5], ar.at[k + 5], at_x(shift(x, d, 4))
+            )
+            for k, d in enumerate((1, -1))
+        ]
+
+    def far_quarter_on():
+        arrived(far_quarter())
+        go(far_quarter_relays())
+
     offs = (0, -1, 1, 2)
     xd_y = [
         Ring(y, at_y, lambda o, part, s=s: xd.at[shift(y, o, 4), shift(x, s, 4), own_half(part)], ys.at[k], yr.at[k])
         for k, s in enumerate(offs)
     ]
-    xu_x = Ring(x, at_x, lambda o, part: xu.at[y, shift(x, o, 4), own_half(part)], xs.at[0], xr.at[0])
+    first_cols, last_cols = pl.ds(0, 512), pl.ds(512, 256)
+    xu_x = Ring(x, at_x, lambda o, part: xu.at[y, shift(x, o, 4), own_half(part), first_cols], xs.at[0], xr.at[0])
     xu_y = [
         Ring(
             y, at_y, lambda o, part, j=j: xu.at[shift(y, o, 4), slots(part), :, pl.ds(j * 256, 256)],
             ys.at[4 + j], yr.at[4 + j],
         )
-        for j in range(3)
+        for j in range(2)
     ]
+    last_y = Ring(y, at_y, lambda o, part: xu.at[shift(y, o, 4), x, own_half(part), last_cols], ys.at[6], yr.at[6])
+    last_x = Ring(x, at_x, lambda o, part: xu.at[slots(part), shift(x, o, 4), :, last_cols], xs.at[2], xr.at[2])
 
     yd_x = Ring(
         x, at_x,
-        lambda o, part: yt.at[0, half_rows(shift(x, o, 4) * MD, MD, part), tokens_of(z)],
+        lambda o, part: yt.at[0, half_rows(shift(x, o, 4) * MD, XFIRST, part), tokens_of(z)],
         xs.at[1], xr.at[1],
     )
     other = at_core(1 - core)
     yd_z = [
         Ring(
             z, at_z,
-            lambda o, part, s=s: yt.at[0, half_rows(shift(x, s, 4) * MD, MD, part), tokens_of(shift(z, o, 4))],
+            lambda o, part, s=s: yt.at[0, half_rows(shift(x, s, 4) * MD, XFIRST, part), tokens_of(shift(z, o, 4))],
             zs.at[k], zr.at[k], other,
+        )
+        for k, s in enumerate(offs)
+    ]
+    rest = MD - XFIRST
+    rest_z = Ring(
+        z, at_z,
+        lambda o, part: yt.at[0, half_rows(x * MD + XFIRST, rest, part), tokens_of(shift(z, o, 4))],
+        xs.at[3], xr.at[3],
+    )
+    rest_x = [
+        Ring(
+            x, at_x,
+            lambda o, part, s=s: yt.at[0, half_rows(shift(x, o, 4) * MD + XFIRST, rest, part), tokens_of(shift(z, s, 4))],
+            zs.at[8 + k], zr.at[8 + k], other,
         )
         for k, s in enumerate(offs)
     ]
     yu_z = [
         Ring(
-            z, at_z, lambda o, part, j=j: yt.at[1, half_rows(j * 512, 512, part), tokens_of(shift(z, o, 4))],
+            z, at_z,
+            lambda o, part, m=m, n=n: yt.at[1, half_rows(m, n, part), tokens_of(shift(z, o, 4))],
             zs.at[4 + j], zr.at[4 + j], other,
         )
-        for j in range(3)
+        for j, (m, n) in enumerate(UP_GROUPS)
     ]
 
     def xchg(buf, n, me, where, send, recv):
@@ -258,14 +309,17 @@
         xs_ = xref[:, :, :, pl.ds(pl.multiple_of(n0, 128), 256)].reshape(T, 256)
         return jnp.dot(yt[which, pl.ds(pl.multiple_of(m0, 128), tm), :], xs_, preferred_element_type=F32)
 
-    def up(m, n):
-        @pl.loop(0, 2)
+    def up(j, n):
+        start, size = UP_GROUPS[j]
+        tm = 256 if size % 256 == 0 else size
+
+        @pl.loop(0, size // tm)
         def _(k):
-            rows, cols = pl.ds(pl.multiple_of(m * 512 + k * 256, 128), 256), pl.ds(n * 256, 256)
-            g = product(1, xu, m * 512 + k * 256, 256, n * 256)
+            rows, cols = pl.ds(pl.multiple_of(start + k * tm, 128), tm), pl.ds(n * 256, 256)
+            g = product(1, xu, start + k * tm, tm, n * 256)
             gu[rows, cols] = g
             prod = g * wu[rows, cols].astype(F32)
-            gwacc[0] += jnp.sum(prod.reshape(32, 8, 256), axis=0)
+            gwacc[0] += jnp.sum(prod.reshape(tm // 8, 8, 256), axis=0)
 
     def out_copies(o):
         if o == 2:
@@ -309,97 +363,58 @@
                 gwacc[1] += acc[:, 0:256] + acc[:, 256:512] + acc[:, 512:768]
 
     gwacc[...] = jnp.zeros_like(gwacc)
+
+    def loaded(*which):
+        for k in which:
+            loads[k].wait()
+
+    def turn_down():
+        loaded(4)
+        yt[0, pl.ds(pl.multiple_of(x * MD, 128), MD), tokens_of(z)] = ystage[:, MU:].T
+
+    def turn_up():
+        loaded(5)
+        for s in range(0, MU, 384):
+            yt[1, s : s + 384, tokens_of(z)] = ystage[:, s : s + 384].T
+
+    acts = {
+        "q13": lambda: go([quarter(1), quarter(3)]),
+        "q13w": lambda: arrived([quarter(1), quarter(3)]),
+        "q2": lambda: go(far_quarter()),
+        "q2f": far_quarter_on,
+        "q2w": lambda: arrived(far_quarter_relays()),
+        "turnU": turn_up,
+        "pass_on": pass_on,
+        "inner_down": inner_down,
+    }
+    for k, o in enumerate((0, 1, 2, -1)):
+        acts[f"down{k}"] = lambda o=o: down(o)
+    for j in range(len(UP_GROUPS)):
+        for n in range(3):
+            acts[f"up{j}_{n}"] = lambda j=j, n=n: up(j, n)
+    for it in range(ITERS):
+        acts[f"s_send{it}"] = lambda it=it: s_send(it)
+        acts[f"s_z{it}"] = lambda it=it: s_z(it)
+        acts[f"t_x{it}"] = lambda it=it: t_x(it)
+        acts[f"t_y{it}"] = lambda it=it: t_y(it)
+    acts["t_fin1"] = lambda: t_fin(1)
+    rings = {"xux": xu_x, "ydx": yd_x, "by": last_y, "bx": last_x, "dz": rest_z}
+    for name, group in (("xd", xd_y), ("yu", xu_y), ("zd", yd_z), ("zu", yu_z), ("dw", rest_x)):
+        for k, r in enumerate(group):
+            rings[f"{name}{k}"] = r
+    for name, r in rings.items():
+        acts[name + "_f"] = r.full
+        acts[name + "_h"] = r.half
+        acts[name + "_d"] = r.done
+        acts[name + "_n"] = r.fin
+
+    turn_down()
+    loaded(2, 3)
     pl.semaphore_wait(barrier, 13)
-    go([quarter(1), quarter(3)])
-    loads[4].wait()
-    yt[0, pl.ds(pl.multiple_of(x * MD, 128), MD), tokens_of(z)] = ystage[:, MU:].T
-    yd_x.full()
-    yd_z[0].full()
-    loads[2].wait()
-    xd_y[0].full()
-    go([quarter(2)])
-    loads[0].wait()
-    loads[1].wait()
-    s_send(0)
-    loads[5].wait()
-    for s in range(0, MU, 384):
-        yt[1, s : s + 384, tokens_of(z)] = ystage[:, s : s + 384].T
-    arrived([quarter(1), quarter(3)])
-    xd_y[1].full()
-    yd_x.half()
-    yd_z[1].full()
-    xd_y[0].half()
-    yd_z[0].half()
-    s_z(0)
-    xd_y[2].full()
-    yd_z[2].full()
-    loads[3].wait()
-    xu_x.full()
-    xd_y[1].half()
-    yd_z[1].half()
-    xd_y[0].done()
-    yd_z[0].done()
-    t_x(0)
-    arrived([quarter(2)])
-    xd_y[3].full()
-    yd_x.done()
-    yd_z[3].full()
-    xd_y[2].half()
-    yd_z[2].half()
-    xd_y[1].done()
-    yd_z[1].done()
-    t_y(0)
-    xu_x.half()
-    xu_x.done()
-    xu_y[0].full()
-    yu_z[0].full()
-    xd_y[3].half()
-    yd_z[3].half()
-    xd_y[2].done()
-    yd_z[2].done()
-    s_send(1)
-    s_z(1)
-    xu_y[1].full()
-    yu_z[1].full()
-    xd_y[3].done()
-    yd_z[3].done()
-    for r in yd_z:
-        r.fin()
-    xu_y[0].half()
-    yu_z[0].half()
-    down(2)
-    t_x(1)
-    down(1)
-    down(-1)
-    xu_y[2].full()
-    yu_z[2].full()
-    t_y(1)
-    down(0)
-    pass_on()
-    xu_y[1].half()
-    yu_z[1].half()
-    xu_y[0].done()
-    yu_z[0].done()
-    yu_z[0].fin()
-    up(0, 0)
-    t_fin(1)
-    xu_y[2].half()
-    yu_z[2].half()
-    xu_y[1].done()
-    yu_z[1].done()
-    yu_z[1].fin()
-    up(0, 1)
-    up(1, 1)
-    up(1, 0)
-    inner_down()
-    xu_y[2].done()
-    yu_z[2].done()
-    up(0, 2)
-    up(1, 2)
-    yu_z[2].fin()
-    up(2, 0)
-    up(2, 1)
-    up(2, 2)
+    for name in ORDER:
+        if name == "s_send0":
+            loaded(0, 1)
+        acts[name]()
 
     squares = get(f_t, 8, state["t"])
     gw = jnp.concatenate(
@@ -486,6 +501,7 @@
             pltpu.VMEM((MD, ND), BF16),
             pltpu.VMEM((3, MD, Q), BF16),
             pltpu.VMEM((2, MD // 2, Q), BF16),
+            pltpu.VMEM((2, TOK // 2, Q), BF16),
             pltpu.VMEM((2, 8, 256), F32),
             pltpu.VMEM((ITERS, 2, 1, MALL), F32),
             pltpu.VMEM((ITERS, 4, 1, MALL), F32),
@@ -496,14 +512,14 @@
             pltpu.VMEM((4, 1, 256), F32),
             pltpu.VMEM((8, 1, 256), F32),
             dma((6,)),
-            dma((3,)),
-            dma((3,)),
-            dma((2, 4)),
-            dma((2, 4)),
+            dma((7,)),
+            dma((7,)),
+            dma((4, 4)),
+            dma((4, 4)),
             dma((7, 4)),
             dma((7, 4)),
-            dma((7, 8)),
-            dma((7, 8)),
+            dma((12, 8)),
+            dma((12, 8)),
             dma((6,)),
             dma((6,)),
             dma((ITERS, 4, 3)),

time: 123 us -> 109 us (0.89)
  Pallas kernels: 122 us -> 108 us
    pallas_call x1, Pallas kernels: 118 us -> 104 us  [local(): pl.pallas_call(kernel, out_shape=(pltpu.VMEM((MU, NU), F32), pltpu.VMEM((...]
where the time goes in v3:
time: 109 us
  Pallas kernels  108 us (99%)
    pallas_call x1, Pallas kernels, local(): pl.pallas_call(kernel, out_shape=(pltpu.VMEM((MU, NU), F32), pltpu.VMEM((...  104 us
    pallas_call x1, Pallas kernels, local(): pl.pallas_call(scale, out_shape=(jax.ShapeDtypeStruct((MU, NU), BF16), ja...  4.02 us

profile of v3, /device:TPU:1, one launch (start us, length us, event | category | flops | bytes accessed | tf_op | source)
XLA Modules:
  0.0 108.8 jit_solution(12596394686973403174)
XLA Ops:
  0.6 0.0 copy-start
  0.6 104.0 %shard_map.144 = (f32[1536,768]{1,0:T(8,128)S(1)}, bf16[4,384,768]{2,1,0:T(8,128)(2,1)S(1)}, f32[1920,128]{1,0:T(8,128)S(1)}, f32[1,1920]{1,0:T(1,128)S(1)}, f32...) custom-call(bf16[1536,768]{1,0:T(8,128)(2,1)} %wu_h.1, bf16[384,3072]{1,0:T(8,128)(2,1)} %wd_h.1, bf16[192,768]{1,0:T(8,128)(2,1)} %xu_h.1, ...), custom_call_target="tpu_custom_call" | custom-call | tf_op jit(solution)/shard_map/pallas_call | solution.py:483
  104.6 0.0 copy-done
  104.6 4.0 %shard_map.145 = (bf16[1536,768]{1,0:T(8,128)(2,1)}, bf16[384,3072]{1,0:T(8,128)(2,1)}, f32[2]{0:T(128)}, f32[1536]{0:T(1024)}, f32[768]{0:T(1024)}, /*index=5*/f32[384]{0:T(512)}, f32[3072]{0:T(1024)}) custom-call(f32[2]{0:T(128)S(1)} %copy-done, f32[1536,768]{1,0:T(8,128)S(1)} %get-tuple-element.13.gu, bf16[4,384,768]{2,1,0:T(8,128)(2,1)S(1)} %get-tuple-element.14.gdown, ...), custom_call_target="tpu_custom_call" | custom-call | tf_op jit(solution)/shard_map/pallas_call | solution.py:535
Async XLA Ops:
  0.6 104.0 %copy-start = (f32[2]{0:T(128)S(1)}, f32[2]{0:T(128)}, u32[]{:S(2)}) copy-start(f32[2]{0:T(128)} %gain.1) | copy-start | bytes 28
